TPU v7x, 512 devices: a whole 4x4x16 slice. The times are simulated.
512 devices in a mesh: wide: 32 (over x, z_hi, core), narrow: 16 (over y, z_lo).
Axes of the slice: x: 4, y: 4, z: 16 (z_hi: 4, z_lo: 4; z = z_hi * 4 + z_lo), core: 2. Of those that a mesh axis runs over, the one named last changes fastest.
Arguments:
- features: bfloat16 [262144, 512], P(('wide', 'narrow')), may hold values from -6 to 6
- stripe_owner: int32 [16, 2], replicated, may hold values from 0 to 31
- dense_weight: int32 [262144, 1024], P(('wide', 'narrow')), may hold values from 0 to 3
- sparse_weight: int32 [512, 16, 128, 128], P(('wide', 'narrow')), may hold values from 0 to 3
- send_blocks: int32 [512, 16, 2], P(('wide', 'narrow')), may hold values from -1 to 3, as said below
- target_block: int32 [512, 16, 2], P(('wide', 'narrow')), may hold values from 0 to 3
- first_weight: bfloat16 [512, 2048], P('wide'), may hold values from -0.25 to 0.25
- second_weight: bfloat16 [2048, 512], P('wide'), may hold values from -0.125 to 0.125
Outputs:
- updated: bfloat16 [262144, 512], P(('wide', 'narrow'))
Inputs may be any that keep to these rules, and one draw needn't show every extreme that they name: `send_blocks`: entry [d, p, s] names a local row block of device d for slot s to partition p of d's wide group, -1 marks an empty slot, filled slots come first; in every wide group one partition receives 2 blocks from every member.
All inputs are finite; a program needn't handle non-finite values.
Results may differ from a plain program's by a relative error of at most 0.0057.
Values may be sent and summed in bfloat16 or wider, within the bound.
A program may use at most 128 MiB of HBM per device.

v0:
```python
import jax
import jax.numpy as jnp
from jax import lax
from jax.sharding import PartitionSpec as P


def padded_to(lines, count):
    spare = -len(lines) % count
    return jnp.pad(lines, [(0, spare)] + [(0, 0)] * (lines.ndim - 1))


def total_of(x, axis):
    lines = x.reshape(-1, *x.shape[1:][-1:])
    padded = padded_to(lines, lax.axis_size(axis))
    own = lax.psum_scatter(padded, axis, scatter_dimension=0, tiled=True)
    whole = lax.all_gather(own, axis, axis=0, tiled=True)
    return whole[: len(lines)].reshape(x.shape)


def tile_products(tile_weights, received):
    carried, present = received
    products = jnp.einsum(
        "pij,pcjd->pcid", tile_weights, carried, preferred_element_type=jnp.float32
    )
    return (products, present)


def add_rows(left, portion):
    return jnp.dot(left, portion, preferred_element_type=jnp.float32)


def shards(
    features,
    stripe_owner,
    dense_weight,
    sparse_weight,
    send_blocks,
    target_block,
    first_weight,
    second_weight,
):
    row_count, feature_width = features.shape
    block_rows = sparse_weight.shape[2]
    blocks_dev = row_count // block_rows
    stripe_count = stripe_owner.shape[1]
    narrow_index = lax.axis_index("narrow")
    wide_index = lax.axis_index("wide")
    owners = lax.dynamic_index_in_dim(stripe_owner, narrow_index, 0, keepdims=False)
    wide_rows = features.astype(jnp.float32)
    masked = jnp.stack(
        [
            jnp.where(owners[stripe_index] == wide_index, wide_rows, 0.0)
            for stripe_index in range(stripe_count)
        ]
    )
    stripes = (
        total_of(masked.astype(jnp.bfloat16), "wide")
        .astype(jnp.float32)
        .astype(jnp.bfloat16)
        .reshape(stripe_count * row_count, feature_width)
    )
    dense_sum = jnp.dot(
        dense_weight.astype(jnp.bfloat16), stripes, preferred_element_type=jnp.float32
    )
    tile_weights = sparse_weight[0].astype(jnp.bfloat16)
    listed = send_blocks[0]
    present = listed >= 0
    block_grid = features.reshape(blocks_dev, block_rows, feature_width)
    chosen = jnp.take(block_grid, jnp.maximum(listed, 0), axis=0)
    chosen = jnp.where(present[:, :, None, None], chosen, jnp.zeros((), jnp.bfloat16))
    products, arrived = tile_products(
        tile_weights,
        (
            lax.all_to_all(chosen, "narrow", split_axis=0, concat_axis=0, tiled=True),
            lax.all_to_all(
                present.astype(jnp.bfloat16), "narrow", split_axis=0, concat_axis=0, tiled=True
            ),
        ),
    )
    highest = lax.Precision.HIGHEST
    routed = (target_block[0][:, :, None] == jnp.arange(blocks_dev)[None, None, :]) & (
        arrived[:, :, None] > 0.5
    )
    routed = routed.astype(jnp.float32)
    sparse_sum = jnp.einsum("pcb,pcid->bid", routed, products, precision=highest).reshape(
        row_count, feature_width
    )
    row_weight = jnp.sum(sparse_weight[0], axis=2).astype(jnp.float32)
    sparse_degree = jnp.einsum("pcb,pi->bi", routed, row_weight, precision=highest).reshape(
        row_count
    )
    degree = 1.0 + jnp.sum(dense_weight, axis=1).astype(jnp.float32) + sparse_degree
    combined = (
        features.astype(jnp.float32) + (dense_sum + sparse_sum) / jnp.sqrt(degree)[:, None]
    ).astype(jnp.bfloat16)
    gated = add_rows(combined, lax.all_gather(first_weight, "wide", axis=0, tiled=True))
    hidden = jax.nn.relu(gated).astype(jnp.bfloat16)
    updated = add_rows(hidden, lax.all_gather(second_weight, "wide", axis=0, tiled=True))
    return updated.astype(jnp.bfloat16)


def solution(mesh):
    placed = (
        P(("wide", "narrow"), None),
        P(),
        P(("wide", "narrow"), None),
        P(("wide", "narrow"), None, None, None),
        P(("wide", "narrow"), None, None),
        P(("wide", "narrow"), None, None),
        P("wide", None),
        P("wide", None),
    )
    return jax.shard_map(
        shards, mesh=mesh, in_specs=placed, out_specs=P(("wide", "narrow"), None), check_vma=False
    )
```

profile of v0, /device:TPU:6, one launch (start us, length us, event | category | flops | bytes accessed | tf_op | source)
XLA Modules:
  0.0 397.5 jit_solution(15326536748898205373)
XLA Ops:
  6.5 0.7 convert_bitcast_fusion
  7.2 0.7 copy.38
  7.9 8.6 %all-to-all-start = ((bf16[16,1,2]{2,1,0:T(2,128)(2,1)}), bf16[16,1,2]{2,1,0:T(2,128)(2,1)S(1)}, u32[]{:S(2)}, u32[]{:S(2)}) async-start(bf16[16,1,2]{2,1,0:T(2,128)(2,1)} %copy.38), calls=%async_computation.1 | async-start | bytes 16384 | tf_op jit(solution)/shard_map/all_to_all | solution.py:75
  16.6 0.7 broadcast_maximum_fusion
  17.3 0.1 copy.40
  17.4 0.1 copy.41
  17.5 0.1 copy.42
  17.5 0.1 reshape.93
  17.6 3.8 gather_fusion
  21.4 6.4 %copy.43 = bf16[32,128,512]{1,2,0:T(8,128)(2,1)} copy(bf16[32,128,512]{2,1,0:T(8,128)(2,1)} %gather_fusion) | data formatting | bytes 8388608 | tf_op jit(solution)/shard_map/jit(_take)/gather | solution.py:69
  27.9 4.7 %select_select_fusion = bf16[16,2,128,512]{2,3,1,0:T(8,128)(2,1)} fusion(bf16[16,2,128,512]{2,3,1,0:T(8,128)(2,1)} %bitcast.57, pred[16,2]{1,0:T(8,128)(4,1)S(1)} %copy.41, pred[16,2]{1,0:T(8,128)(4,1)S(1)} %copy.40), kind=kLoop, calls=%fused_computation.2 | loop fusion | flops 4194304 | bytes 8388672 | tf_op jit(solution)/shard_map/jit(_where)/select_n | solution.py:70
  32.6 0.0 all-to-all-done
  32.6 7.7 %all-to-all-start.1 = ((bf16[16,2,128,512]{2,3,1,0:T(8,128)(2,1)}), bf16[16,2,128,512]{2,3,1,0:T(8,128)(2,1)}, u32[]{:S(2)}, u32[]{:S(2)}) async-start(bf16[16,2,128,512]{2,3,1,0:T(8,128)(2,1)} %select_select_fusion), calls=%async_computation.2 | async-start | bytes 8388608 | tf_op jit(solution)/shard_map/all_to_all | solution.py:74
  40.3 0.0 copy-start.2
  40.3 0.0 reduce-scatter.2.cloned.1.call-start
  40.3 0.2 copy.36
  40.6 0.0 copy-start.4
  40.6 0.0 copy-done
  40.6 0.1 constant_dynamic-slice_fusion
  40.7 0.7 fusion.20
  42.5 0.2 fusion.9
  42.7 0.0 copy-start.5
  42.7 0.1 pad_maximum_fusion
  42.8 1.3 copy.37
  44.2 0.0 reduce-scatter.2.cloned.1.call-update
  44.2 0.0 all-gather.4.cloned.1.call-start
  44.2 118.9 %reduce-scatter.2.cloned.1.call-done = bf16[32,512]{1,0:T(8,128)(2,1)} async-done(((bf16[1024,512]{1,0:T(8,128)(2,1)}), bf16[32,512]{1,0:T(8,128)(2,1)}) %reduce-scatter.2.cloned.1.call-update) | async-done | bytes 32784 | tf_op jit(solution)/shard_map/reduce_scatter | solution.py:15
  163.2 0.0 all-gather.4.cloned.1.call-update
  163.2 0.0 all-gather.6.cloned.1.call-start
  163.2 0.7 all-gather.6.cloned.1.call-update
  163.9 0.0 all-gather.8.cloned.1.call-start
  164.0 0.5 all-gather.8.cloned.1.call-update
  164.5 0.3 reduce_sum.29
  164.9 1.8 reduce_sum.27
  166.6 0.1 copy.39
  166.8 0.1 fusion.4
  166.9 0.0 all-to-all-done.1
  166.9 6.7 %convolution_bitcast_fusion = f32[16,2,128,512]{2,3,1,0:T(8,128)} fusion(bf16[16,2,128,512]{2,3,1,0:T(8,128)(2,1)} %all-to-all-done.1, s32[1,16,128,128]{3,2,1,0:T(8,128)S(1)} %copy-done.2), kind=kOutput, calls=%fused_computation.3 | convolution fusion | flops 537133056 | bytes 13631488 | tf_op jit(solution)/shard_map/pij,pcjd->pcid/dot_general | solution.py:22
  173.6 10.4 %copy.44 = f32[16,2,128,512]{3,0,1,2:T(8,128)} copy(f32[16,2,128,512]{2,3,1,0:T(8,128)} %convolution_bitcast_fusion) | data formatting | bytes 16777216 | tf_op jit(solution)/shard_map/pij,pcjd->pcid/transpose | solution.py:22
  184.0 5.6 %convolution_bitcast_fusion.1 = f32[4,128,512]{2,0,1:T(4,128)S(1)} fusion(f32[16,2,128,512]{3,0,1,2:T(8,128)} %copy.44, s32[16,2]{0,1:T(2,128)S(1)} %bitcast.61, pred[16,2]{0,1:T(4,128)(4,1)S(1)} %compare_bitcast_fusion.1), kind=kOutput, calls=%fused_computation.7 | convolution fusion | flops 100663552 | bytes 9437344 | tf_op jit(solution)/shard_map/pcb,pcid->bid/dot_general | solution.py:85
  189.6 0.0 copy-start.3
  189.6 0.3 copy.45
  189.9 1.3 copy.46
  191.2 41.0 %all-gather.4.cloned.1.call-done = bf16[1024,512]{1,0:T(8,128)(2,1)} async-done(((bf16[32,512]{1,0:T(8,128)(2,1)}), bf16[1024,512]{1,0:T(8,128)(2,1)}) %all-gather.4.cloned.1.call-update) | async-done | bytes 1048592 | tf_op jit(solution)/shard_map/all_gather | solution.py:16
  232.3 2.5 fusion.2
  234.7 74.8 %all-gather.6.cloned.1.call-done = bf16[512,2048]{1,0:T(8,128)(2,1)} async-done(((bf16[16,2048]{1,0:T(8,128)(2,1)}), bf16[512,2048]{1,0:T(8,128)(2,1)}) %all-gather.6.cloned.1.call-update) | async-done | bytes 2097168 | tf_op jit(solution)/shard_map/all_gather | solution.py:96
  309.6 76.0 %all-gather.8.cloned.1.call-done = bf16[2048,512]{1,0:T(8,128)(2,1)} async-done(((bf16[64,512]{1,0:T(8,128)(2,1)}), bf16[2048,512]{1,0:T(8,128)(2,1)}) %all-gather.8.cloned.1.call-update) | async-done | bytes 2097168 | tf_op jit(solution)/shard_map/all_gather | solution.py:98
  385.6 5.4 %convolution_convert_fusion = bf16[512,512]{1,0:T(8,128)(2,1)} fusion(bf16[2048,512]{1,0:T(8,128)(2,1)} %all-gather.8.cloned.1.call-done, bf16[512,512]{0,1:T(8,128)(2,1)S(1)} %fusion.2, bf16[512,2048]{1,0:T(8,128)(2,1)} %all-gather.6.cloned.1.call-done), kind=kOutput, calls=%fused_computation.11 | convolution fusion | flops 2149842944 | bytes 5242880 | tf_op jit(solution)/shard_map/dot_general | solution.py:29
  (10 shorter events, 0.0 us)
Async XLA Ops:
  6.5 34.0 %copy-start = (s32[16,2]{0,1:T(2,128)S(1)}, s32[16,2]{0,1:T(2,128)}, u32[]{:S(2)}) copy-start(s32[16,2]{0,1:T(2,128)} %param.9) | copy-start | bytes 388
  7.9 24.6 %all-to-all-start = ((bf16[16,1,2]{2,1,0:T(2,128)(2,1)}), bf16[16,1,2]{2,1,0:T(2,128)(2,1)S(1)}, u32[]{:S(2)}, u32[]{:S(2)}) async-start(bf16[16,1,2]{2,1,0:T(2,128)(2,1)} %copy.38), calls=%async_computation.1 | async-start | bytes 16384 | tf_op jit(solution)/shard_map/all_to_all | solution.py:75
  32.6 7.8 %copy-start.1 = (bf16[512,512]{1,0:T(8,128)(2,1)S(1)}, bf16[512,512]{1,0:T(8,128)(2,1)}, u32[]{:S(2)}) copy-start(bf16[512,512]{1,0:T(8,128)(2,1)} %param.8) | copy-start | bytes 1572868
  32.6 134.3 %all-to-all-start.1 = ((bf16[16,2,128,512]{2,3,1,0:T(8,128)(2,1)}), bf16[16,2,128,512]{2,3,1,0:T(8,128)(2,1)}, u32[]{:S(2)}, u32[]{:S(2)}) async-start(bf16[16,2,128,512]{2,3,1,0:T(8,128)(2,1)} %select_select_fusion), calls=%async_computation.2 | async-start | bytes 8388608 | tf_op jit(solution)/shard_map/all_to_all | solution.py:74
  40.3 124.3 %copy-start.2 = (s32[1,16,128,128]{3,2,1,0:T(8,128)S(1)}, s32[1,16,128,128]{3,2,1,0:T(8,128)}, u32[]{:S(2)}) copy-start(s32[1,16,128,128]{3,2,1,0:T(8,128)} %param.11) | copy-start | bytes 3145732
  40.3 122.9 %reduce-scatter.2.cloned.1.call-start = ((), (), s32[]{:S(2)}) async-start(), calls=%async_computation.3 | async-start | bytes 1081344 | tf_op jit(solution)/shard_map/reduce_scatter | solution.py:15
  40.6 2.2 copy-start.4
  42.7 124.0 %copy-start.5 = (s32[1,16,2]{1,2,0:T(2,128)S(1)}, s32[1,16,2]{1,2,0:T(2,128)}, u32[]{:S(2)}) copy-start(s32[1,16,2]{1,2,0:T(2,128)} %param.13) | copy-start | bytes 388
  44.2 188.1 %all-gather.4.cloned.1.call-start = ((), (), s32[]{:S(2)}) async-start(), calls=%async_computation.4 | async-start | bytes 1081344 | tf_op jit(solution)/shard_map/all_gather | solution.py:16
  163.2 146.4 %all-gather.6.cloned.1.call-start = ((), (), s32[]{:S(2)}) async-start(), calls=%async_computation.5 | async-start | bytes 2162688 | tf_op jit(solution)/shard_map/all_gather | solution.py:96
  163.9 221.6 %all-gather.8.cloned.1.call-start = ((), (), s32[]{:S(2)}) async-start(), calls=%async_computation.6 | async-start | bytes 2162688 | tf_op jit(solution)/shard_map/all_gather | solution.py:98
  189.6 42.7 %copy-start.3 = (s32[512,1024]{1,0:T(8,128)S(1)}, s32[512,1024]{1,0:T(8,128)}, u32[]{:S(2)}) copy-start(s32[512,1024]{1,0:T(8,128)} %param.10) | copy-start | bytes 6291460
Sparse Core Ops, SparseCore 0:
  45.4 117.6 reduce-scatter.1
  166.3 65.9 all-gather.3
  235.4 74.1 all-gather.5
  312.6 72.9 all-gather.7
where the time goes:
time: 400 us; the launch traced here: 397 us
  waiting for transfers between devices  312 us (78%)
  local copies, waits for them, and re-layouts  25.7 us (6%)
  matrix products  20.3 us (5%)
  starting transfers between devices  16.5 us (4%)
  between operations  14.5 us (4%)
  other arithmetic  8.46 us (2%)
    reduce_scatter x1, waiting for transfers between devices, total_of(): own = lax.psum_scatter(padded, axis, scatter_dimension=0, tiled=True)  119 us
    all_gather x1, waiting for transfers between devices, shards(): lax.all_gather(second_weight, 'wide', axis=0, tiled=True)  76 us
    all_gather x1, waiting for transfers between devices, shards(): lax.all_gather(first_weight, 'wide', axis=0, tiled=True)  74.8 us
    all_gather x1, waiting for transfers between devices, total_of(): whole = lax.all_gather(own, axis, axis=0, tiled=True)  41 us
    transpose x1, local copies, waits for them, and re-layouts, tile_products(): jnp.einsum('pij,pcjd->pcid', tile_weights, carried, preferred_element_typ...  10.4 us
    gather x2, local copies, waits for them, and re-layouts, shards(): chosen = jnp.take(block_grid, jnp.maximum(listed, 0), axis=0)  10.2 us
    all_to_all x1, starting transfers between devices, shards(): lax.all_to_all(present.astype(jnp.bfloat16), 'narrow', split_axis=0, conc...  8.64 us
  transfers between devices with their start and end apart: 6, of which 4 were waited for; matrix products, arithmetic and copies ran while one was open for 12% of the time, Pallas kernels for 0%

commit v1 on v0

v1 whole, which is shorter than its diff:
```python
import jax
import jax.numpy as jnp
from jax import lax
from jax.experimental import pallas as pl
from jax.experimental.pallas import tpu as pltpu
from jax.sharding import PartitionSpec as P

MESH = pl.DeviceIdType.MESH
BF = jnp.bfloat16
F32 = jnp.float32
N_SEND = 128
N_RECV = 128


def kernel(
    owner_ref, target_ref, f_ref, flag_ref, w1_in, w2_in, dense_hbm, tile_hbm, out_ref,
    zf, fl, gate, tx, fwd, got_x, route, w1, w2, partner_f, cand, rxh, rxp, candz, rzh, rzp,
    stripes, dense, tiles, dense16, acc, deg, comb, send_sem, recv_sem, load_sem,
):
    w, n = lax.axis_index("wide"), lax.axis_index("narrow")
    x, h, c = lax.div(w, 8), lax.rem(lax.div(w, 2), 4), lax.rem(w, 2)
    y, i = lax.div(n, 4), lax.rem(n, 4)

    def up(v, by=1):
        return lax.rem(v + by, 4)

    def at(xx=x, hh=h, cc=c, yy=y, ii=i):
        return {"wide": xx * 8 + hh * 2 + cc, "narrow": yy * 4 + ii}

    x_r, x_l, x_o = up(x), up(x, 3), up(x, 2)
    h_r, h_l, h_o = up(h), up(h, 3), up(h, 2)
    y_r, y_l, y_o = up(y), up(y, 3), up(y, 2)
    right_x, left_x = at(xx=x_r), at(xx=x_l)
    right_h, left_h = at(hh=h_r), at(hh=h_l)
    right_y, left_y, far_y = at(yy=y_r), at(yy=y_l), at(yy=y_o)
    partner = at(cc=1 - c)
    z = h * 4 + i
    z_r, z_l = lax.rem(z + 1, 16), lax.rem(z + 15, 16)
    right_z = at(hh=lax.div(z_r, 4), ii=lax.rem(z_r, 4))
    left_z = at(hh=lax.div(z_l, 4), ii=lax.rem(z_l, 4))
    line = [at(ii=up(i, k)) for k in (1, 2, 3)]

    pending = []
    count = {"send": 0, "recv": 0}

    def slots(kind, k=1):
        count[kind] += k
        return count[kind] - k

    def send(src, dst, recv, device, cond=None):
        slot = slots("send")

        def copy():
            return pltpu.make_async_remote_copy(
                src_ref=src, dst_ref=dst, send_sem=send_sem.at[slot], recv_sem=recv_sem.at[recv],
                device_id=device, device_id_type=MESH,
            )

        if cond is None:
            copy().start()
        else:
            pl.when(cond)(lambda: copy().start())
        pending.append((copy, cond))

    def arrived(dst, recv):
        pltpu.make_async_remote_copy(
            src_ref=dst, dst_ref=dst, send_sem=send_sem.at[0], recv_sem=recv_sem.at[recv],
            device_id=partner, device_id_type=MESH,
        ).wait_recv()

    loads = [
        pltpu.make_async_copy(dense_hbm, dense, load_sem.at[0]),
        pltpu.make_async_copy(tile_hbm, tiles, load_sem.at[1]),
    ]
    for load in loads:
        load.start()
    barrier = pltpu.get_barrier_semaphore()
    peers = [right_x, left_x, right_h, left_h, right_y, left_y, far_y, partner, right_z, left_z, *line]
    for peer in peers:
        pl.semaphore_signal(barrier, inc=1, device_id=peer, device_id_type=MESH)
    fl[n] = flag_ref[...]
    acc[...] = jnp.zeros_like(acc)
    pl.semaphore_wait(barrier, len(peers))

    r_flag = slots("recv", 4)
    r_flag_y = slots("recv", 4)
    r_f = slots("recv", 4)
    r_part = slots("recv")
    r_swap = slots("recv")
    r_y = slots("recv", 24)
    r_chain = slots("recv", 6)
    r_wx = slots("recv", 24)
    r_wc = slots("recv", 8)
    r_s = slots("recv", 16)

    def load_own_weights():
        pass

    def w_own():
        for part, (src, buf) in enumerate(((w1_in, w1), (w2_in, w2))):
            send(src, buf.at[x, h, c], r_chain + part, right_z, i == 3)
            send(src, buf.at[x, h, c], r_chain + 2 + part, left_z, i == 0)

    def w_x_own():
        for part, (src, buf) in enumerate(((w1_in, w1), (w2_in, w2))):
            send(src, buf.at[x, h, c], r_wx + part, right_x)
            send(src, buf.at[x, h, c], r_wx + 2 + part, left_x)

    def chain_near(position):
        @pl.when(i == position)
        def _():
            arrived(w1.at[x, h_l, c], r_chain + 0)
            arrived(w2.at[x, h_l, c], r_chain + 1)

        near_l = i == position
        near_r = i == 3 - position
        if position < 3:
            send(w1.at[x, h_l, c], w1.at[x, h_l, c], r_chain + 0, right_z, near_l)
            send(w2.at[x, h_l, c], w2.at[x, h_l, c], r_chain + 1, right_z, near_l)
        else:
            send(w1.at[x, h_l, c], w1.at[x, h_l, c], r_chain + 4, right_z, near_l)

        @pl.when(near_r)
        def _():
            arrived(w1.at[x, h_r, c], r_chain + 2)
            arrived(w2.at[x, h_r, c], r_chain + 3)

        if position < 3:
            send(w1.at[x, h_r, c], w1.at[x, h_r, c], r_chain + 2, left_z, near_r)
            send(w2.at[x, h_r, c], w2.at[x, h_r, c], r_chain + 3, left_z, near_r)
        else:
            send(w2.at[x, h_r, c], w2.at[x, h_r, c], r_chain + 5, left_z, near_r)

    def chain_far(position):
        near_l = i == position
        near_r = i == 3 - position

        @pl.when(near_l)
        def _():
            arrived(w1.at[x, h_o, c], r_chain + 4)

        if position < 3:
            send(w1.at[x, h_o, c], w1.at[x, h_o, c], r_chain + 4, right_z, near_l)

        @pl.when(near_r)
        def _():
            arrived(w2.at[x, h_o, c], r_chain + 5)

        if position < 3:
            send(w2.at[x, h_o, c], w2.at[x, h_o, c], r_chain + 5, left_z, near_r)

    def w_x(group, hh):
        base = r_wx + 6 * group
        for part, buf in enumerate((w1, w2)):
            send(buf.at[x, hh, c], buf.at[x, hh, c], base + part, right_x)
            send(buf.at[x, hh, c], buf.at[x, hh, c], base + 2 + part, left_x)

    def w_x_relay(group, hh):
        base = r_wx + 6 * group
        arrived(w1.at[x_l, hh, c], base + 0)
        send(w1.at[x_l, hh, c], w1.at[x_l, hh, c], base + 4, right_x)
        arrived(w2.at[x_r, hh, c], base + 3)
        send(w2.at[x_r, hh, c], w2.at[x_r, hh, c], base + 5, left_x)

    def w_x_done(group, hh):
        base = r_wx + 6 * group
        arrived(w2.at[x_l, hh, c], base + 1)
        arrived(w1.at[x_r, hh, c], base + 2)
        arrived(w1.at[x_o, hh, c], base + 4)
        arrived(w2.at[x_o, hh, c], base + 5)
        send(w1.at[:, hh, c], w1.at[:, hh, c], r_wc + 2 * group, partner)
        send(w2.at[:, hh, c], w2.at[:, hh, c], r_wc + 2 * group + 1, partner)

    def w_core(group, hh):
        arrived(w1.at[:, hh, 1 - c], r_wc + 2 * group)
        arrived(w2.at[:, hh, 1 - c], r_wc + 2 * group + 1)

    def s_start():
        send(f_ref, partner_f, r_part, partner)

    def s_mask():
        owner = owner_ref[c, n]
        mine = jnp.where(owner == w, 1.0, 0.0)
        other = jnp.where(owner == w + 1 - 2 * c, 1.0, 0.0)
        arrived(partner_f, r_part)
        for q in range(4):
            rows = pl.ds(q * 128, 128)
            cand[q] = (f_ref[rows, :].astype(F32) * mine + partner_f[rows, :].astype(F32) * other).astype(BF)

    def rs_first(buf, half, me_o, rbuf, base, right, left):
        send(buf.at[me_o, pl.ds(0, half)], rbuf.at[0], base + 0, right)
        send(buf.at[me_o, pl.ds(half, half)], rbuf.at[1], base + 1, left)

    def rs_second(buf, half, me_r, me_l, rbuf, pbuf, base, right, left):
        arrived(rbuf.at[0], base + 0)
        buf[me_r, 0:half] = buf[me_r, 0:half] + rbuf[0]
        arrived(rbuf.at[1], base + 1)
        buf[me_l, half:] = buf[me_l, half:] + rbuf[1]
        send(buf.at[me_r], pbuf.at[0], base + 2, right)
        send(buf.at[me_l], pbuf.at[1], base + 3, left)

    def s_x1():
        rs_first(cand, 64, x_o, rxh, r_s + 0, right_x, left_x)

    def s_x2():
        rs_second(cand, 64, x_r, x_l, rxh, rxp, r_s + 0, right_x, left_x)

    def s_z1():
        arrived(rxp.at[0], r_s + 2)
        arrived(rxp.at[1], r_s + 3)
        candz[...] = (cand[x] + rxp[0] + rxp[1]).reshape(4, 32, 512)
        rs_first(candz, 16, h_o, rzh, r_s + 4, right_h, left_h)

    def s_z2():
        rs_second(candz, 16, h_r, h_l, rzh, rzp, r_s + 4, right_h, left_h)

    def s_z3():
        arrived(rzp.at[0], r_s + 6)
        arrived(rzp.at[1], r_s + 7)
        stripes[c, x, h] = candz[h] + rzp[0] + rzp[1]
        piece = stripes.at[c, x, h]
        send(piece, piece, r_s + 8, right_h)
        send(piece, piece, r_s + 9, left_h)

    def s_z4():
        arrived(stripes.at[c, x, h_l], r_s + 8)
        half = stripes.at[c, x, h_l, pl.ds(0, 16)]
        send(half, half, r_s + 10, right_h)
        arrived(stripes.at[c, x, h_r], r_s + 9)
        half = stripes.at[c, x, h_r, pl.ds(16, 16)]
        send(half, half, r_s + 11, left_h)

    def s_x3():
        arrived(stripes.at[c, x, h_o, pl.ds(0, 16)], r_s + 10)
        arrived(stripes.at[c, x, h_o, pl.ds(16, 16)], r_s + 11)
        piece = stripes.at[c, x]
        send(piece, piece, r_s + 12, right_x)
        send(piece, piece, r_s + 13, left_x)

    def s_x4():
        arrived(stripes.at[c, x_l], r_s + 12)
        half = stripes.at[c, x_l, pl.ds(0, 2)]
        send(half, half, r_s + 14, right_x)
        arrived(stripes.at[c, x_r], r_s + 13)
        half = stripes.at[c, x_r, pl.ds(2, 2)]
        send(half, half, r_s + 15, left_x)

    def s_swap():
        arrived(stripes.at[c, x_o, pl.ds(0, 2)], r_s + 14)
        arrived(stripes.at[c, x_o, pl.ds(2, 2)], r_s + 15)
        send(stripes.at[c], stripes.at[c], r_swap, partner)

    def s_done():
        arrived(stripes.at[1 - c], r_swap)

    def flags_z():
        for k in (1, 2, 3):
            send(flag_ref, fl.at[n], r_flag + i, line[k - 1])

    def flags_y():
        for k in (1, 2, 3):
            j = up(i, k)
            arrived(fl.at[y * 4 + j], r_flag + j)
        row = fl.at[pl.ds(y * 4, 4)]
        for device in (right_y, left_y, far_y):
            send(row, row, r_flag_y + y, device)

    def flags_done():
        for k in (1, 2, 3):
            yy = up(y, k)
            arrived(fl.at[pl.ds(yy * 4, 4)], r_flag_y + yy)

    first = jnp.where(i == 0, 1, i - 1)
    second = jnp.where(i == 0, 2, jnp.where(i == 1, 2, jnp.where(i == 2, 3, 1)))
    third = jnp.where(i < 2, 3, 0)
    order = [i, first, second, third]

    def f_own():
        send(f_ref, zf.at[i], r_f + i, right_z, i < 3)
        send(f_ref, zf.at[i], r_f + i, left_z, i > 0)

    def f_relay(k):
        j = order[k]
        arrived(zf.at[j], r_f + j)
        send(zf.at[j], zf.at[j], r_f + j, right_z, (j < i) & (i < 3))
        send(zf.at[j], zf.at[j], r_f + j, left_z, (j > i) & (i > 0))

    def pick(k):
        j = order[k]
        source = f_ref if k == 0 else zf.at[j]
        tile = fl[y * 4 + j]
        lane = lax.broadcasted_iota(jnp.int32, (8, 128), 1)
        for d in range(4):
            column = up(y, d) * 4 + i
            value = jnp.sum(jnp.where(lane == column, tile, 0.0), axis=1, keepdims=True)
            for s in range(2):
                one = jnp.broadcast_to(value[s : s + 1, :], (16, 128))
                for e in range(4):
                    gate[(d * 2 + s) * 4 + e] = jnp.where(one == e + 1.0, 1.0, 0.0).astype(BF)

        @pl.loop(0, 8)
        def _(r):
            blocks = [source[pl.ds(pl.multiple_of(e * 128 + r * 16, 16), 16), :] for e in range(4)]
            for d in range(4):
                for s in range(2):
                    total = None
                    for e in range(4):
                        g = gate[(d * 2 + s) * 4 + e]
                        term = blocks[e] * jnp.concatenate([g, g, g, g], axis=1)
                        total = term if total is None else total + term
                    rows = pl.ds(pl.multiple_of(r * 16, 16), 16)
                    if d == 0:
                        got_x[y * 4 + j, s, rows, :] = total
                    else:
                        tx[k, d - 1, s, rows, :] = total

    def y_send(k):
        p = y * 4 + order[k]
        base = r_y + 6 * k
        send(tx.at[k, 1, 0], fwd.at[k, 0], base + 2, right_y)
        send(tx.at[k, 1, 1], fwd.at[k, 1], base + 3, left_y)
        send(tx.at[k, 0], got_x.at[p], base + 0, right_y)
        send(tx.at[k, 2], got_x.at[p], base + 1, left_y)

    def y_relay(k):
        base = r_y + 6 * k
        arrived(fwd.at[k, 0], base + 2)
        send(fwd.at[k, 0], got_x.at[y_l * 4 + order[k], 0], base + 4, right_y)
        arrived(fwd.at[k, 1], base + 3)
        send(fwd.at[k, 1], got_x.at[y_r * 4 + order[k], 1], base + 5, left_y)

    def y_done(k):
        base = r_y + 6 * k
        arrived(got_x.at[y_l * 4 + order[k]], base + 0)
        arrived(got_x.at[y_r * 4 + order[k]], base + 1)
        arrived(got_x.at[y_o * 4 + order[k], 0], base + 4)
        arrived(got_x.at[y_o * 4 + order[k], 1], base + 5)

    def prepare():
        for load in loads:
            load.wait()
        for q in range(4):
            rows = pl.ds(q * 128, 128)
            block = dense[rows, :]
            dense16[rows, :] = block.astype(F32).astype(BF)
            total = 1.0 + jnp.sum(block.astype(F32), axis=1, keepdims=True)
            deg[rows, :] = jnp.broadcast_to(total, (128, 128))

        @pl.loop(0, 16)
        def _(p):
            tile = tiles[p].astype(F32)
            for s in range(2):
                for b in range(4):
                    hit = jnp.where(target_ref[s, p] == b, 1.0, 0.0)
                    route[p, pl.ds(b * 128, 128), pl.ds(s * 128, 128)] = (tile * hit).astype(BF)

    def degrees():
        lane = lax.broadcasted_iota(jnp.int32, (8, 128), 1)

        @pl.loop(0, 16)
        def _(p):
            rows = jnp.sum(tiles[p].astype(F32), axis=1, keepdims=True)
            value = jnp.sum(jnp.where(lane == n, fl[p], 0.0), axis=1, keepdims=True)
            present = jnp.minimum(value, 1.0)
            for b in range(4):
                weight = jnp.zeros((1, 1), F32)
                for s in range(2):
                    hit = jnp.where(target_ref[s, p] == b, 1.0, 0.0)
                    weight = weight + present[s : s + 1, :] * hit
                where = pl.ds(b * 128, 128)
                deg[where, :] = deg[where, :] + jnp.broadcast_to(rows * weight, (128, 128))

    def sparse(k):
        @pl.loop(0, 4)
        def _(yy):
            p = yy * 4 + order[k]
            block = got_x[p].reshape(256, 512)
            acc[...] += jnp.dot(route[p], block, preferred_element_type=F32)

    def dense_part():
        for k in range(2):
            block = stripes[k].reshape(512, 512)
            acc[...] += jnp.dot(dense16[:, k * 512 : (k + 1) * 512], block, preferred_element_type=F32)

    def combine():
        for q in range(4):
            rows = pl.ds(q * 128, 128)
            scale = 1.0 / jnp.sqrt(deg[rows, :])
            scale = jnp.concatenate([scale, scale, scale, scale], axis=1)
            comb[rows, :] = (f_ref[rows, :].astype(F32) + acc[rows, :] * scale).astype(BF)

    def mlp():
        acc[...] = jnp.zeros_like(acc)

        @pl.loop(0, 4)
        def _(q):
            left = w1[:, :, :, :, pl.ds(pl.multiple_of(q * 512, 512), 512)].reshape(512, 512)
            hidden = jnp.dot(comb[...], left, preferred_element_type=F32)
            hidden = jnp.maximum(hidden, 0.0).astype(BF)
            acc[...] += jnp.dot(hidden, w2[q].reshape(512, 512), preferred_element_type=F32)

        out_ref[...] = acc[...].astype(BF)

    s_start()
    flags_z()
    w_own()
    w_x_own()
    f_own()
    pick(0)
    y_send(0)
    w1[x, h, c] = w1_in[...]
    w2[x, h, c] = w2_in[...]
    s_mask()
    s_x1()
    flags_y()
    w_x_relay(0, h)
    s_x2()
    chain_near(0)
    prepare()
    y_relay(0)
    s_z1()
    f_relay(1)
    pick(1)
    y_send(1)
    chain_near(1)
    s_z2()
    w_x_done(0, h)
    chain_near(2)
    y_relay(1)
    s_z3()
    f_relay(2)
    pick(2)
    y_send(2)
    flags_done()
    degrees()
    y_done(0)
    sparse(0)
    chain_near(3)
    w_x(1, h_l)
    w_x(2, h_r)
    s_z4()
    chain_far(0)
    y_relay(2)
    f_relay(3)
    pick(3)
    y_send(3)
    chain_far(1)
    s_x3()
    w_x_relay(1, h_l)
    w_x_relay(2, h_r)
    chain_far(2)
    y_done(1)
    sparse(1)
    s_x4()
    chain_far(3)
    w_x(3, h_o)
    w_x_done(1, h_l)
    w_x_done(2, h_r)
    s_swap()
    w_x_relay(3, h_o)
    y_relay(3)
    y_done(2)
    sparse(2)
    w_x_done(3, h_o)
    s_done()
    dense_part()
    y_done(3)
    sparse(3)
    combine()
    for group, hh in enumerate((h, h_l, h_r, h_o)):
        w_core(group, hh)
    mlp()
    for copy, cond in pending:
        if cond is None:
            copy().wait_send()
        else:
            pl.when(cond)(lambda copy=copy: copy().wait_send())


def shards(features, stripe_owner, dense_weight, sparse_weight, send_blocks, target_block, first_weight, second_weight):
    flags = jnp.pad((send_blocks[0].T + 1).astype(F32), ((0, 6), (0, 112)))
    smem = pl.BlockSpec(memory_space=pltpu.SMEM)
    vmem = pl.BlockSpec(memory_space=pltpu.VMEM)
    hbm = pl.BlockSpec(memory_space=pl.ANY)
    return pl.pallas_call(
        kernel,
        out_shape=jax.ShapeDtypeStruct((512, 512), BF),
        in_specs=[smem, smem, vmem, vmem, vmem, vmem, hbm, hbm],
        out_specs=vmem,
        scratch_shapes=[
            pltpu.VMEM((4, 512, 512), BF),
            pltpu.VMEM((16, 8, 128), F32),
            pltpu.VMEM((32, 16, 128), BF),
            pltpu.VMEM((4, 3, 2, 128, 512), BF),
            pltpu.VMEM((4, 2, 128, 512), BF),
            pltpu.VMEM((16, 2, 128, 512), BF),
            pltpu.VMEM((16, 512, 256), BF),
            pltpu.VMEM((4, 4, 2, 16, 2048), BF),
            pltpu.VMEM((4, 4, 2, 64, 512), BF),
            pltpu.VMEM((512, 512), BF),
            pltpu.VMEM((4, 128, 512), BF),
            pltpu.VMEM((2, 64, 512), BF),
            pltpu.VMEM((2, 128, 512), BF),
            pltpu.VMEM((4, 32, 512), BF),
            pltpu.VMEM((2, 16, 512), BF),
            pltpu.VMEM((2, 32, 512), BF),
            pltpu.VMEM((2, 4, 4, 32, 512), BF),
            pltpu.VMEM((512, 1024), jnp.int32),
            pltpu.VMEM((16, 128, 128), jnp.int32),
            pltpu.VMEM((512, 1024), BF),
            pltpu.VMEM((512, 512), F32),
            pltpu.VMEM((512, 128), F32),
            pltpu.VMEM((512, 512), BF),
            pltpu.SemaphoreType.DMA((N_SEND,)),
            pltpu.SemaphoreType.DMA((N_RECV,)),
            pltpu.SemaphoreType.DMA((2,)),
        ],
        compiler_params=pltpu.CompilerParams(
            collective_id=0, has_side_effects=True, vmem_limit_bytes=56 * 2**20
        ),
    )(stripe_owner.T, target_block[0].T, features, flags, first_weight, second_weight, dense_weight, sparse_weight[0])


def solution(mesh):
    placed = (
        P(("wide", "narrow"), None),
        P(),
        P(("wide", "narrow"), None),
        P(("wide", "narrow"), None, None, None),
        P(("wide", "narrow"), None, None),
        P(("wide", "narrow"), None, None),
        P("wide", None),
        P("wide", None),
    )
    return jax.shard_map(
        shards, mesh=mesh, in_specs=placed, out_specs=P(("wide", "narrow"), None), check_vma=False
    )
```

time: 400 us -> 103 us (0.26)
  waiting for transfers between devices: 312 us -> 0 us
  Pallas kernels: 0 us -> 99.4 us
  local copies, waits for them, and re-layouts: 25.7 us -> 2.47 us
  matrix products: 20.3 us -> 0 us
  starting transfers between devices: 16.5 us -> 0 us
  between operations: 14.5 us -> 0.01 us
  other arithmetic: 8.46 us -> 0.68 us
    all_gather x3 -> x0, waiting for transfers between devices: 192 us -> none  [the longest x1 76 us: shards(): lax.all_gather(second_weight, 'wide', axis=0, tiled=True)]
    reduce_scatter x1 -> x0, waiting for transfers between devices: 119 us -> none  [total_of(): own = lax.psum_scatter(padded, axis, scatter_dimension=0, tiled=True)]
    pallas_call x0 -> x1, Pallas kernels: none -> 99.4 us  [shards(): pl.pallas_call(kernel, out_shape=jax.ShapeDtypeStruct((512, 512), BF), in...]
    dot_general x5 -> x0, matrix products: 20.3 us -> none  [the longest x1 6.68 us: tile_products(): jnp.einsum('pij,pcjd->pcid', tile_weights, carried, preferred_element_typ...]
    all_to_all x2 -> x0, starting transfers between devices: 16.3 us -> none  [the longest x1 8.64 us: shards(): lax.all_to_all(present.astype(jnp.bfloat16), 'narrow', split_axis=0, conc...]
    transpose x1 -> x0, local copies, waits for them, and re-layouts: 10.4 us -> none  [tile_products(): jnp.einsum('pij,pcjd->pcid', tile_weights, carried, preferred_element_typ...]
    gather x2 -> x0, local copies, waits for them, and re-layouts: 10.2 us -> none  [shards(): chosen = jnp.take(block_grid, jnp.maximum(listed, 0), axis=0)]
    select_n x1 -> x0, other arithmetic: 4.66 us -> none  [shards(): jnp.where(present[:, :, None, None], chosen, jnp.zeros((), jnp.bfloat16))]
  transfers between devices with their start and end apart: 6 -> 0, of which waited for: 4 -> 0; matrix products, arithmetic and copies ran while one was open for 12% -> 0% of each run, Pallas kernels for 0% -> 0%
where the time goes in v1:
time: 103 us
  Pallas kernels  99.4 us (97%)
  local copies, waits for them, and re-layouts  2.47 us (2%)
    pallas_call x1, Pallas kernels, shards(): pl.pallas_call(kernel, out_shape=jax.ShapeDtypeStruct((512, 512), BF), in...  99.4 us

profile of v1, /device:TPU:6, one launch (start us, length us, event | category | flops | bytes accessed | tf_op | source)
XLA Modules:
  0.0 102.5 jit_solution(12620528902944328870)
XLA Ops:
  0.0 0.7 convert_bitcast_fusion
  0.7 0.6 pad.4.flag_ref
  1.3 99.4 %shard_map.82 = bf16[512,512]{1,0:T(8,128)(2,1)} custom-call(s32[2,16]{1,0:T(2,128)} %bitcast.10, s32[2,16]{1,0:T(2,128)} %bitcast.11, bf16[512,512]{1,0:T(8,128)(2,1)} %f_ref.1, f32[8,128]{1,0:T(8,128)} %pad.4.flag_ref, bf16[16,2048]{1,0:T(8,128)(2,1)} %w1_in.1, bf16[64,512]{1,0:T(8,128)(2,1)} %w2_in.1, s32[512,1024]{1,0:T(8,128)} %dense_hbm.1, ...), custom_call_target="tpu_custom_call" | custom-call | tf_op jit(solution)/shard_map/pallas_call | solution.py:485
  100.6 1.9 %copy.10 = bf16[512,512]{1,0:T(8,128)(2,1)} copy(bf16[512,512]{1,0:T(8,128)(2,1)} %shard_map.82) | data formatting | bytes 1048576

commit v2 on v1

--- a/solution.py
+++ b/solution.py
@@ -8,13 +8,13 @@
 MESH = pl.DeviceIdType.MESH
 BF = jnp.bfloat16
 F32 = jnp.float32
-N_SEND = 128
+N_SEND = 192
 N_RECV = 128
 
 
 def kernel(
-    owner_ref, target_ref, f_ref, flag_ref, w1_in, w2_in, dense_hbm, tile_hbm, out_ref,
-    zf, fl, gate, tx, fwd, got_x, route, w1, w2, partner_f, cand, rxh, rxp, candz, rzh, rzp,
+    owner_ref, target_ref, f_ref, list_ref, w1_in, w2_in, dense_hbm, tile_hbm, out_ref,
+    zf, fl, gate, tx, got_x, route, w1, w2, partner_f, cand, rxh, rxp, candz, rzh, rzp,
     stripes, dense, tiles, dense16, acc, deg, comb, send_sem, recv_sem, load_sem,
 ):
     w, n = lax.axis_index("wide"), lax.axis_index("narrow")
@@ -34,10 +34,9 @@
     right_h, left_h = at(hh=h_r), at(hh=h_l)
     right_y, left_y, far_y = at(yy=y_r), at(yy=y_l), at(yy=y_o)
     partner = at(cc=1 - c)
-    z = h * 4 + i
-    z_r, z_l = lax.rem(z + 1, 16), lax.rem(z + 15, 16)
-    right_z = at(hh=lax.div(z_r, 4), ii=lax.rem(z_r, 4))
-    left_z = at(hh=lax.div(z_l, 4), ii=lax.rem(z_l, 4))
+    right_z, left_z = at(ii=up(i)), at(ii=up(i, 3))
+    low_end, high_end = i == 0, i == 3
+    end, middle = low_end | high_end, (i == 1) | (i == 2)
     line = [at(ii=up(i, k)) for k in (1, 2, 3)]
 
     pending = []
@@ -61,6 +60,33 @@
         else:
             pl.when(cond)(lambda: copy().start())
         pending.append((copy, cond))
+
+    def send_apart(src, dst, cut, recv, device, cond=None):
+        slot = slots("send")
+        size = src.shape[0]
+
+        def copy(lo, hi):
+            part = pl.ds(lo, hi - lo)
+            return pltpu.make_async_remote_copy(
+                src_ref=src.at[part], dst_ref=dst.at[part], send_sem=send_sem.at[slot], recv_sem=recv_sem.at[recv],
+                device_id=device, device_id_type=MESH,
+            )
+
+        def start():
+            @pl.when(c == 0)
+            def _():
+                copy(0, size).start()
+
+            @pl.when(c == 1)
+            def _():
+                copy(0, cut).start()
+                copy(cut, size).start()
+
+        if cond is None:
+            start()
+        else:
+            pl.when(cond)(start)
+        pending.append((lambda: copy(0, size), cond))
 
     def arrived(dst, recv):
         pltpu.make_async_remote_copy(
@@ -75,79 +101,69 @@
     for load in loads:
         load.start()
     barrier = pltpu.get_barrier_semaphore()
-    peers = [right_x, left_x, right_h, left_h, right_y, left_y, far_y, partner, right_z, left_z, *line]
-    for peer in peers:
+    peers = [right_x, left_x, right_h, left_h, right_y, left_y, far_y, partner, *line]
+    for peer in [*peers, at(hh=h_l, ii=3), at(hh=h_r, ii=0)]:
         pl.semaphore_signal(barrier, inc=1, device_id=peer, device_id_type=MESH)
-    fl[n] = flag_ref[...]
+    fl[n] = jnp.zeros((8, 128), F32)
+    fl[n, 0:2, 0:16] = (list_ref[...] + 1).astype(F32)
     acc[...] = jnp.zeros_like(acc)
-    pl.semaphore_wait(barrier, len(peers))
+    pl.semaphore_wait(barrier, len(peers) + jnp.where(end, 4, 0))
 
     r_flag = slots("recv", 4)
     r_flag_y = slots("recv", 4)
-    r_f = slots("recv", 4)
+    r_f = slots("recv", 8)
     r_part = slots("recv")
     r_swap = slots("recv")
-    r_y = slots("recv", 24)
+    r_y = slots("recv", 32)
     r_chain = slots("recv", 6)
     r_wx = slots("recv", 24)
     r_wc = slots("recv", 8)
     r_s = slots("recv", 16)
 
-    def load_own_weights():
-        pass
-
-    def w_own():
-        for part, (src, buf) in enumerate(((w1_in, w1), (w2_in, w2))):
-            send(src, buf.at[x, h, c], r_chain + part, right_z, i == 3)
-            send(src, buf.at[x, h, c], r_chain + 2 + part, left_z, i == 0)
+    def w_near(to_right, to_left, away):
+        own = ((w1_in, w1), (w2_in, w2))
+        for part in to_right:
+            send(own[part][0], own[part][1].at[x, h, c], r_chain + part, at(hh=h_r, ii=away), high_end)
+        for part in to_left:
+            send(own[part][0], own[part][1].at[x, h, c], r_chain + 2 + part, at(hh=h_l, ii=3 - away), low_end)
+
+    def w_far(away):
+        send(w1.at[x, h_l, c], w1.at[x, h_l, c], r_chain + 4, at(hh=h_r, ii=away), high_end)
+        send(w2.at[x, h_r, c], w2.at[x, h_r, c], r_chain + 5, at(hh=h_l, ii=3 - away), low_end)
+
+    def w_far_got():
+        @pl.when(high_end)
+        def _():
+            arrived(w1.at[x, h_l, c], r_chain + 0)
+
+        @pl.when(low_end)
+        def _():
+            arrived(w2.at[x, h_r, c], r_chain + 3)
+
+    lower = i < 2
+    h_a, h_b = jnp.where(lower, h_l, h_r), jnp.where(lower, h_r, h_l)
+
+    def w_a_done():
+        arrived(w1.at[x, h_a, c], r_chain + jnp.where(lower, 0, 2))
+        arrived(w2.at[x, h_a, c], r_chain + jnp.where(lower, 1, 3))
+
+    def w_b_done():
+        @pl.when(jnp.logical_not(high_end))
+        def _():
+            arrived(w1.at[x, h_b, c], r_chain + jnp.where(lower, 2, 0))
+
+        @pl.when(jnp.logical_not(low_end))
+        def _():
+            arrived(w2.at[x, h_b, c], r_chain + jnp.where(lower, 3, 1))
+
+    def w_far_done():
+        arrived(w1.at[x, h_o, c], r_chain + 4)
+        arrived(w2.at[x, h_o, c], r_chain + 5)
 
     def w_x_own():
         for part, (src, buf) in enumerate(((w1_in, w1), (w2_in, w2))):
             send(src, buf.at[x, h, c], r_wx + part, right_x)
             send(src, buf.at[x, h, c], r_wx + 2 + part, left_x)
-
-    def chain_near(position):
-        @pl.when(i == position)
-        def _():
-            arrived(w1.at[x, h_l, c], r_chain + 0)
-            arrived(w2.at[x, h_l, c], r_chain + 1)
-
-        near_l = i == position
-        near_r = i == 3 - position
-        if position < 3:
-            send(w1.at[x, h_l, c], w1.at[x, h_l, c], r_chain + 0, right_z, near_l)
-            send(w2.at[x, h_l, c], w2.at[x, h_l, c], r_chain + 1, right_z, near_l)
-        else:
-            send(w1.at[x, h_l, c], w1.at[x, h_l, c], r_chain + 4, right_z, near_l)
-
-        @pl.when(near_r)
-        def _():
-            arrived(w1.at[x, h_r, c], r_chain + 2)
-            arrived(w2.at[x, h_r, c], r_chain + 3)
-
-        if position < 3:
-            send(w1.at[x, h_r, c], w1.at[x, h_r, c], r_chain + 2, left_z, near_r)
-            send(w2.at[x, h_r, c], w2.at[x, h_r, c], r_chain + 3, left_z, near_r)
-        else:
-            send(w2.at[x, h_r, c], w2.at[x, h_r, c], r_chain + 5, left_z, near_r)
-
-    def chain_far(position):
-        near_l = i == position
-        near_r = i == 3 - position
-
-        @pl.when(near_l)
-        def _():
-            arrived(w1.at[x, h_o, c], r_chain + 4)
-
-        if position < 3:
-            send(w1.at[x, h_o, c], w1.at[x, h_o, c], r_chain + 4, right_z, near_l)
-
-        @pl.when(near_r)
-        def _():
-            arrived(w2.at[x, h_o, c], r_chain + 5)
-
-        if position < 3:
-            send(w2.at[x, h_o, c], w2.at[x, h_o, c], r_chain + 5, left_z, near_r)
 
     def w_x(group, hh):
         base = r_wx + 6 * group
@@ -255,7 +271,7 @@
 
     def flags_z():
         for k in (1, 2, 3):
-            send(flag_ref, fl.at[n], r_flag + i, line[k - 1])
+            send(fl.at[n], fl.at[n], r_flag + i, line[k - 1])
 
     def flags_y():
         for k in (1, 2, 3):
@@ -275,20 +291,27 @@
     third = jnp.where(i < 2, 3, 0)
     order = [i, first, second, third]
 
-    def f_own():
-        send(f_ref, zf.at[i], r_f + i, right_z, i < 3)
-        send(f_ref, zf.at[i], r_f + i, left_z, i > 0)
-
-    def f_relay(k):
+    def f_own(half):
+        source = f_ref.at[:, pl.ds(half * 256, 256)]
+        send(source, zf.at[i, half], r_f + i * 2 + half, right_z, i < 3)
+        send(source, zf.at[i, half], r_f + i * 2 + half, left_z, i > 0)
+
+    def f_got(k, half, cond=None):
+        def wait():
+            arrived(zf.at[order[k], half], r_f + order[k] * 2 + half)
+
+        if cond is None:
+            wait()
+        else:
+            pl.when(cond)(wait)
+
+    def f_relay(k, half):
         j = order[k]
-        arrived(zf.at[j], r_f + j)
-        send(zf.at[j], zf.at[j], r_f + j, right_z, (j < i) & (i < 3))
-        send(zf.at[j], zf.at[j], r_f + j, left_z, (j > i) & (i > 0))
-
-    def pick(k):
-        j = order[k]
-        source = f_ref if k == 0 else zf.at[j]
-        tile = fl[y * 4 + j]
+        send(zf.at[j, half], zf.at[j, half], r_f + j * 2 + half, right_z, (j < i) & (i < 3))
+        send(zf.at[j, half], zf.at[j, half], r_f + j * 2 + half, left_z, (j > i) & (i > 0))
+
+    def gates(k):
+        tile = fl[y * 4 + order[k]]
         lane = lax.broadcasted_iota(jnp.int32, (8, 128), 1)
         for d in range(4):
             column = up(y, d) * 4 + i
@@ -298,43 +321,48 @@
                 for e in range(4):
                     gate[(d * 2 + s) * 4 + e] = jnp.where(one == e + 1.0, 1.0, 0.0).astype(BF)
 
+    def pick(k, half):
+        j = order[k]
+
         @pl.loop(0, 8)
         def _(r):
-            blocks = [source[pl.ds(pl.multiple_of(e * 128 + r * 16, 16), 16), :] for e in range(4)]
+            blocks = []
+            for e in range(4):
+                rows = pl.ds(pl.multiple_of(e * 128 + r * 16, 16), 16)
+                blocks.append(f_ref[rows, half * 256 : half * 256 + 256] if k == 0 else zf[j, half, rows, :])
+            rows = pl.ds(pl.multiple_of(r * 16, 16), 16)
             for d in range(4):
                 for s in range(2):
                     total = None
                     for e in range(4):
                         g = gate[(d * 2 + s) * 4 + e]
-                        term = blocks[e] * jnp.concatenate([g, g, g, g], axis=1)
+                        term = blocks[e] * jnp.concatenate([g, g], axis=1)
                         total = term if total is None else total + term
-                    rows = pl.ds(pl.multiple_of(r * 16, 16), 16)
                     if d == 0:
-                        got_x[y * 4 + j, s, rows, :] = total
+                        got_x[k, half, 0, s, rows, :] = total
+                    elif d == 2:
+                        tx[k, half, s, 2, rows, :] = total
                     else:
-                        tx[k, d - 1, s, rows, :] = total
-
-    def y_send(k):
-        p = y * 4 + order[k]
-        base = r_y + 6 * k
-        send(tx.at[k, 1, 0], fwd.at[k, 0], base + 2, right_y)
-        send(tx.at[k, 1, 1], fwd.at[k, 1], base + 3, left_y)
-        send(tx.at[k, 0], got_x.at[p], base + 0, right_y)
-        send(tx.at[k, 2], got_x.at[p], base + 1, left_y)
-
-    def y_relay(k):
-        base = r_y + 6 * k
-        arrived(fwd.at[k, 0], base + 2)
-        send(fwd.at[k, 0], got_x.at[y_l * 4 + order[k], 0], base + 4, right_y)
-        arrived(fwd.at[k, 1], base + 3)
-        send(fwd.at[k, 1], got_x.at[y_r * 4 + order[k], 1], base + 5, left_y)
-
-    def y_done(k):
-        base = r_y + 6 * k
-        arrived(got_x.at[y_l * 4 + order[k]], base + 0)
-        arrived(got_x.at[y_r * 4 + order[k]], base + 1)
-        arrived(got_x.at[y_o * 4 + order[k], 0], base + 4)
-        arrived(got_x.at[y_o * 4 + order[k], 1], base + 5)
+                        tx[k, half, d // 2, s, rows, :] = total
+
+    def y_send(k, half):
+        base = r_y + 8 * k + 4 * half
+        for way, device in enumerate((right_y, left_y)):
+            if k == 0 and half == 0:
+                send_apart(tx.at[k, half, way], got_x.at[k, half, 1 + way], 1, base + way, device)
+            else:
+                send(tx.at[k, half, way], got_x.at[k, half, 1 + way], base + way, device)
+
+    def y_relay(k, half):
+        base = r_y + 8 * k + 4 * half
+        for way, device in enumerate((right_y, left_y)):
+            arrived(got_x.at[k, half, 1 + way], base + way)
+            send(got_x.at[k, half, 1 + way, 2], got_x.at[k, half, 3, way], base + 2 + way, device)
+
+    def y_done(k, half):
+        base = r_y + 8 * k + 4 * half
+        arrived(got_x.at[k, half, 3, 0], base + 2)
+        arrived(got_x.at[k, half, 3, 1], base + 3)
 
     def prepare():
         for load in loads:
@@ -354,28 +382,26 @@
                     hit = jnp.where(target_ref[s, p] == b, 1.0, 0.0)
                     route[p, pl.ds(b * 128, 128), pl.ds(s * 128, 128)] = (tile * hit).astype(BF)
 
-    def degrees():
-        lane = lax.broadcasted_iota(jnp.int32, (8, 128), 1)
-
-        @pl.loop(0, 16)
-        def _(p):
-            rows = jnp.sum(tiles[p].astype(F32), axis=1, keepdims=True)
-            value = jnp.sum(jnp.where(lane == n, fl[p], 0.0), axis=1, keepdims=True)
-            present = jnp.minimum(value, 1.0)
-            for b in range(4):
-                weight = jnp.zeros((1, 1), F32)
-                for s in range(2):
-                    hit = jnp.where(target_ref[s, p] == b, 1.0, 0.0)
-                    weight = weight + present[s : s + 1, :] * hit
-                where = pl.ds(b * 128, 128)
-                deg[where, :] = deg[where, :] + jnp.broadcast_to(rows * weight, (128, 128))
-
-    def sparse(k):
+    def sparse(k, half, low=0, high=4):
+        columns = slice(half * 256, half * 256 + 256)
+
+        @pl.loop(low, high)
+        def _(source):
+            away = jnp.where(source == 1, 3, jnp.where(source == 2, 1, jnp.where(source == 3, 2, 0)))
+            p = lax.rem(y + away, 4) * 4 + order[k]
+            block = got_x[k, half, source, 0:2].reshape(256, 256)
+            acc[:, columns] += jnp.dot(route[p], block, preferred_element_type=F32)
+
+    def degrees(k):
         @pl.loop(0, 4)
         def _(yy):
             p = yy * 4 + order[k]
-            block = got_x[p].reshape(256, 512)
-            acc[...] += jnp.dot(route[p], block, preferred_element_type=F32)
+            lane = lax.broadcasted_iota(jnp.int32, (8, 128), 1)
+            value = jnp.sum(jnp.where(lane == n, fl[p], 0.0), axis=1, keepdims=True)
+            present = jnp.minimum(value, 1.0)
+            ones = [jnp.broadcast_to(present[s : s + 1, :], (128, 128)) for s in range(2)]
+            ones = jnp.concatenate(ones, axis=0).astype(BF)
+            deg[...] += jnp.dot(route[p], ones, preferred_element_type=F32)
 
     def dense_part():
         for k in range(2):
@@ -401,73 +427,119 @@
 
         out_ref[...] = acc[...].astype(BF)
 
+    both = (0, 1)
     s_start()
     flags_z()
-    w_own()
+    f_own(0)
+    f_own(1)
+    w_near((0,), (1,), 3)
+    w_near(both, both, 0)
+    gates(0)
+    pick(0, 0)
+    y_send(0, 0)
+    pick(0, 1)
+    y_send(0, 1)
+    s_mask()
+    s_x1()
     w_x_own()
-    f_own()
-    pick(0)
-    y_send(0)
     w1[x, h, c] = w1_in[...]
     w2[x, h, c] = w2_in[...]
-    s_mask()
-    s_x1()
     flags_y()
+    s_x2()
+    prepare()
+    f_got(1, 0)
+    f_got(2, 0, middle)
+    gates(1)
+    pick(1, 0)
+    s_z1()
+    f_relay(1, 0)
+    f_relay(2, 0)
+    y_relay(0, 0)
+    y_send(1, 0)
+    w_far_got()
+    w_far(0)
+    w_near(both, both, 1)
+    w_far(1)
+    f_got(1, 1)
+    f_got(2, 1, middle)
+    pick(1, 1)
     w_x_relay(0, h)
-    s_x2()
-    chain_near(0)
-    prepare()
-    y_relay(0)
-    s_z1()
-    f_relay(1)
-    pick(1)
-    y_send(1)
-    chain_near(1)
     s_z2()
+    f_relay(1, 1)
+    f_relay(2, 1)
+    y_relay(0, 1)
+    y_send(1, 1)
+    f_got(2, 0, end)
+    f_got(3, 0, middle)
+    gates(2)
+    pick(2, 0)
+    s_z3()
+    f_relay(3, 0)
+    y_relay(1, 0)
+    y_send(2, 0)
+    w_near(both, both, 2)
+    w_far(2)
+    w_a_done()
+    w_x(1, h_a)
     w_x_done(0, h)
-    chain_near(2)
-    y_relay(1)
-    s_z3()
-    f_relay(2)
-    pick(2)
-    y_send(2)
+    f_got(2, 1, end)
+    f_got(3, 1, middle)
+    pick(2, 1)
+    s_z4()
+    f_relay(3, 1)
+    y_relay(1, 1)
+    y_send(2, 1)
     flags_done()
-    degrees()
-    y_done(0)
-    sparse(0)
-    chain_near(3)
-    w_x(1, h_l)
-    w_x(2, h_r)
-    s_z4()
-    chain_far(0)
-    y_relay(2)
-    f_relay(3)
-    pick(3)
-    y_send(3)
-    chain_far(1)
+    for k in range(4):
+        degrees(k)
+    y_done(0, 0)
+    y_done(0, 1)
+    sparse(0, 0)
+    sparse(0, 1)
+    w_x_relay(1, h_a)
+    f_got(3, 0, end)
+    gates(3)
+    pick(3, 0)
+    y_relay(2, 0)
+    y_send(3, 0)
+    w_near((1,), (0,), 3)
+    w_far(3)
     s_x3()
-    w_x_relay(1, h_l)
-    w_x_relay(2, h_r)
-    chain_far(2)
-    y_done(1)
-    sparse(1)
+    f_got(3, 1, end)
+    pick(3, 1)
+    y_relay(2, 1)
+    y_send(3, 1)
+    y_done(1, 0)
+    y_done(1, 1)
+    sparse(1, 0)
+    sparse(1, 1)
     s_x4()
-    chain_far(3)
+    w_b_done()
+    w_x(2, h_b)
+    w_far_done()
     w_x(3, h_o)
-    w_x_done(1, h_l)
-    w_x_done(2, h_r)
+    w_x_done(1, h_a)
     s_swap()
+    y_relay(3, 0)
+    w_x_relay(2, h_b)
     w_x_relay(3, h_o)
-    y_relay(3)
-    y_done(2)
-    sparse(2)
+    y_done(2, 0)
+    y_done(2, 1)
+    sparse(2, 0)
+    sparse(2, 1)
+    w_x_done(2, h_b)
+    y_relay(3, 1)
     w_x_done(3, h_o)
+    sparse(3, 0, 0, 3)
     s_done()
     dense_part()
-    y_done(3)
-    sparse(3)
+    sparse(3, 1, 0, 3)
+    y_done(3, 0)
+    sparse(3, 0, 3, 4)
+    y_done(3, 1)
+    sparse(3, 1, 3, 4)
     combine()
-    for group, hh in enumerate((h, h_l, h_r, h_o)):
+    for group, hh in enumerate((h, h_a, h_b, h_o)):
         w_core(group, hh)
     mlp()
     for copy, cond in pending:
@@ -478,7 +550,6 @@
 
 
 def shards(features, stripe_owner, dense_weight, sparse_weight, send_blocks, target_block, first_weight, second_weight):
-    flags = jnp.pad((send_blocks[0].T + 1).astype(F32), ((0, 6), (0, 112)))
     smem = pl.BlockSpec(memory_space=pltpu.SMEM)
     vmem = pl.BlockSpec(memory_space=pltpu.VMEM)
     hbm = pl.BlockSpec(memory_space=pl.ANY)
@@ -488,12 +559,11 @@
         in_specs=[smem, smem, vmem, vmem, vmem, vmem, hbm, hbm],
         out_specs=vmem,
         scratch_shapes=[
-            pltpu.VMEM((4, 512, 512), BF),
+            pltpu.VMEM((4, 2, 512, 256), BF),
             pltpu.VMEM((16, 8, 128), F32),
             pltpu.VMEM((32, 16, 128), BF),
-            pltpu.VMEM((4, 3, 2, 128, 512), BF),
-            pltpu.VMEM((4, 2, 128, 512), BF),
-            pltpu.VMEM((16, 2, 128, 512), BF),
+            pltpu.VMEM((4, 2, 2, 3, 128, 256), BF),
+            pltpu.VMEM((4, 2, 4, 3, 128, 256), BF),
             pltpu.VMEM((16, 512, 256), BF),
             pltpu.VMEM((4, 4, 2, 16, 2048), BF),
             pltpu.VMEM((4, 4, 2, 64, 512), BF),
@@ -518,7 +588,7 @@
         compiler_params=pltpu.CompilerParams(
             collective_id=0, has_side_effects=True, vmem_limit_bytes=56 * 2**20
         ),
-    )(stripe_owner.T, target_block[0].T, features, flags, first_weight, second_weight, dense_weight, sparse_weight[0])
+    )(stripe_owner.T, target_block[0].T, features, send_blocks[0].T, first_weight, second_weight, dense_weight, sparse_weight[0])
 
 
 def solution(mesh):

time: 103 us -> 90.9 us (0.88)
  Pallas kernels: 99.4 us -> 88.9 us
    pallas_call x1, Pallas kernels: 99.4 us -> 88.9 us  [shards(): pl.pallas_call(kernel, out_shape=jax.ShapeDtypeStruct((512, 512), BF), in...]
where the time goes in v2:
time: 90.9 us; the launch traced here: 90.7 us
  Pallas kernels  88.9 us (98%)
  local copies, waits for them, and re-layouts  1.87 us (2%)
    pallas_call x1, Pallas kernels, shards(): pl.pallas_call(kernel, out_shape=jax.ShapeDtypeStruct((512, 512), BF), in...  88.9 us
    unnamed x1, local copies, waits for them, and re-layouts  1.87 us

profile of v2, /device:TPU:6, one launch (start us, length us, event | category | flops | bytes accessed | tf_op | source)
XLA Modules:
  0.0 90.7 jit_solution(13499387699952141648)
XLA Ops:
  0.0 88.9 %shard_map.82 = bf16[512,512]{1,0:T(8,128)(2,1)} custom-call(s32[2,16]{1,0:T(2,128)} %bitcast.9, s32[2,16]{1,0:T(2,128)} %bitcast.10, bf16[512,512]{1,0:T(8,128)(2,1)} %f_ref.1, s32[2,16]{1,0:T(2,128)} %bitcast.11, bf16[16,2048]{1,0:T(8,128)(2,1)} %w1_in.1, bf16[64,512]{1,0:T(8,128)(2,1)} %w2_in.1, s32[512,1024]{1,0:T(8,128)} %dense_hbm.1, ...), custom_call_target="tpu_custom_call" | custom-call | tf_op jit(solution)/shard_map/pallas_call | solution.py:556
  88.9 1.9 %copy.10 = bf16[512,512]{1,0:T(8,128)(2,1)} copy(bf16[512,512]{1,0:T(8,128)(2,1)} %shard_map.82) | data formatting | bytes 1048576

commit v3 on v2

--- a/solution.py
+++ b/solution.py
@@ -113,7 +113,7 @@
     r_flag_y = slots("recv", 4)
     r_f = slots("recv", 8)
     r_part = slots("recv")
-    r_swap = slots("recv")
+    r_swap = slots("recv", 4)
     r_y = slots("recv", 32)
     r_chain = slots("recv", 6)
     r_wx = slots("recv", 24)
@@ -252,6 +252,7 @@
         piece = stripes.at[c, x]
         send(piece, piece, r_s + 12, right_x)
         send(piece, piece, r_s + 13, left_x)
+        send(piece, piece, r_swap + 0, partner)
 
     def s_x4():
         arrived(stripes.at[c, x_l], r_s + 12)
@@ -260,14 +261,17 @@
         arrived(stripes.at[c, x_r], r_s + 13)
         half = stripes.at[c, x_r, pl.ds(2, 2)]
         send(half, half, r_s + 15, left_x)
+        send(stripes.at[c, x_l], stripes.at[c, x_l], r_swap + 1, partner)
+        send(stripes.at[c, x_r], stripes.at[c, x_r], r_swap + 2, partner)
 
     def s_swap():
         arrived(stripes.at[c, x_o, pl.ds(0, 2)], r_s + 14)
         arrived(stripes.at[c, x_o, pl.ds(2, 2)], r_s + 15)
-        send(stripes.at[c], stripes.at[c], r_swap, partner)
+        send(stripes.at[c, x_o], stripes.at[c, x_o], r_swap + 3, partner)
 
     def s_done():
-        arrived(stripes.at[1 - c], r_swap)
+        for k, xx in enumerate((x, x_l, x_r, x_o)):
+            arrived(stripes.at[1 - c, xx], r_swap + k)
 
     def flags_z():
         for k in (1, 2, 3):
@@ -425,7 +429,7 @@
             hidden = jnp.maximum(hidden, 0.0).astype(BF)
             acc[...] += jnp.dot(hidden, w2[q].reshape(512, 512), preferred_element_type=F32)
 
-        out_ref[...] = acc[...].astype(BF)
+        out_ref[...] = acc[...]
 
     both = (0, 1)
     s_start()
@@ -458,8 +462,6 @@
     y_send(1, 0)
     w_far_got()
     w_far(0)
-    w_near(both, both, 1)
-    w_far(1)
     f_got(1, 1)
     f_got(2, 1, middle)
     pick(1, 1)
@@ -477,15 +479,15 @@
     f_relay(3, 0)
     y_relay(1, 0)
     y_send(2, 0)
-    w_near(both, both, 2)
-    w_far(2)
-    w_a_done()
-    w_x(1, h_a)
     w_x_done(0, h)
     f_got(2, 1, end)
     f_got(3, 1, middle)
     pick(2, 1)
     s_z4()
+    w_near(both, both, 1)
+    w_far(1)
+    w_near(both, both, 2)
+    w_far(2)
     f_relay(3, 1)
     y_relay(1, 1)
     y_send(2, 1)
@@ -496,12 +498,13 @@
     y_done(0, 1)
     sparse(0, 0)
     sparse(0, 1)
-    w_x_relay(1, h_a)
     f_got(3, 0, end)
     gates(3)
     pick(3, 0)
     y_relay(2, 0)
     y_send(3, 0)
+    w_a_done()
+    w_x(1, h_a)
     w_near((1,), (0,), 3)
     w_far(3)
     s_x3()
@@ -509,6 +512,7 @@
     pick(3, 1)
     y_relay(2, 1)
     y_send(3, 1)
+    w_x_relay(1, h_a)
     y_done(1, 0)
     y_done(1, 1)
     sparse(1, 0)
@@ -555,7 +559,7 @@
     hbm = pl.BlockSpec(memory_space=pl.ANY)
     return pl.pallas_call(
         kernel,
-        out_shape=jax.ShapeDtypeStruct((512, 512), BF),
+        out_shape=jax.ShapeDtypeStruct((512, 512), F32),
         in_specs=[smem, smem, vmem, vmem, vmem, vmem, hbm, hbm],
         out_specs=vmem,
         scratch_shapes=[
@@ -588,7 +592,7 @@
         compiler_params=pltpu.CompilerParams(
             collective_id=0, has_side_effects=True, vmem_limit_bytes=56 * 2**20
         ),
-    )(stripe_owner.T, target_block[0].T, features, send_blocks[0].T, first_weight, second_weight, dense_weight, sparse_weight[0])
+    )(stripe_owner.T, target_block[0].T, features, send_blocks[0].T, first_weight, second_weight, dense_weight, sparse_weight[0]).astype(BF)
 
 
 def solution(mesh):

time: 90.9 us -> 91 us (level)
  other arithmetic: 0 us -> 2.08 us
  local copies, waits for them, and re-layouts: 1.87 us -> 0 us
    convert_element_type x0 -> x1, other arithmetic: none -> 2.08 us  [shards(): return pl.pallas_call(kernel, out_shape=jax.ShapeDtypeStruct((512, 512),...]
    unnamed x1 -> x0, local copies, waits for them, and re-layouts: 1.87 us -> none
where the time goes in v3:
time: 91 us; the launch traced here: 90.7 us
  Pallas kernels  88.6 us (97%)
  other arithmetic  2.08 us (2%)
    pallas_call x1, Pallas kernels, shards(): pl.pallas_call(kernel, out_shape=jax.ShapeDtypeStruct((512, 512), F32), i...  88.6 us
    convert_element_type x1, other arithmetic, shards(): return pl.pallas_call(kernel, out_shape=jax.ShapeDtypeStruct((512, 512),...  2.08 us

profile of v3, /device:TPU:6, one launch (start us, length us, event | category | flops | bytes accessed | tf_op | source)
XLA Modules:
  0.0 90.7 jit_solution(9432670813018913737)
XLA Ops:
  0.0 88.6 %shard_map.82 = f32[512,512]{1,0:T(8,128)} custom-call(s32[2,16]{1,0:T(2,128)} %bitcast.9, s32[2,16]{1,0:T(2,128)} %bitcast.10, bf16[512,512]{1,0:T(8,128)(2,1)} %f_ref.1, s32[2,16]{1,0:T(2,128)} %bitcast.11, bf16[16,2048]{1,0:T(8,128)(2,1)} %w1_in.1, bf16[64,512]{1,0:T(8,128)(2,1)} %w2_in.1, s32[512,1024]{1,0:T(8,128)} %dense_hbm.1, s32[16,128,128]{2,1,0:T(8,128)} %bitcast.8), custom_call_target="tpu_custom_call" | custom-call | tf_op jit(solution)/shard_map/pallas_call | solution.py:560
  88.6 2.1 %convert_element_type.3 = bf16[512,512]{1,0:T(8,128)(2,1)} convert(f32[512,512]{1,0:T(8,128)} %shard_map.82) | non-fusion elementwise | flops 262144 | bytes 1572864 | tf_op jit(solution)/shard_map/convert_element_type | solution.py:595
